TPU v7x, 1024 devices: a whole 4x8x16 slice. The times are simulated.
1024 devices in a mesh: row: 32 (over x, y), col: 32 (over z, core).
Axes of the slice: x: 4, y: 8, z: 16, core: 2. Of those that a mesh axis runs over, the one named last changes fastest.
Arguments:
- x_block: bfloat16 [64, 262144], P(None, ('col', 'row')), may hold values from -6 to 6
- tiles: bfloat16 [24576, 256, 256], P(('row', 'col')), may hold values from -0.078125 to 0.078125
- coords: int32 [24576, 2], P(('row', 'col')), may hold values from 0 to 31, as said below
- counts: int32 [1024], P(('row', 'col')), may hold values from 9 to 24, as said below
Outputs:
- basis: float32 [64, 262144], P(None, ('row', 'col'))
- factor: float32 [64, 64], replicated
Inputs may be any that keep to these rules, and one draw needn't show every extreme that they name: `coords`: column 0 is a tile row below 32, column 1 a tile column below 32; at the device of place p = i * 32 + j, slot 0 names tile row j. `counts`: some device uses all 24 slots.
All inputs are finite; a program needn't handle non-finite values.
Results may differ from a plain program's by a relative error of at most 0.0003.
Values may be sent and summed in bfloat16 or wider, within the bound.
A program may use at most 32 MiB of HBM per device.

v0:
```python
import jax
import jax.numpy as jnp
from jax import lax
from jax.sharding import PartitionSpec as P


def local(x_block, tiles, coords, counts):
    vector_count = x_block.shape[0]
    rows_dev = x_block.shape[1]
    tile_size = tiles.shape[1]
    slot_total = tiles.shape[0]
    row_tiles = rows_dev * lax.axis_size("col") // tile_size
    gathered = lax.all_gather(x_block, "row", axis=1, tiled=True)
    picked = jnp.take(gathered.reshape(vector_count, -1, tile_size), coords[:, 1], axis=1)
    live_slots = jnp.arange(slot_total, dtype=jnp.int32) < counts[0]
    onehot = (
        (coords[:, 0][None, :] == jnp.arange(row_tiles, dtype=jnp.int32)[:, None])
        & live_slots[None, :]
    ).astype(jnp.float32)
    contrib = jnp.einsum("ckj,kij->kci", picked, tiles, preferred_element_type=jnp.float32)
    summed = jnp.einsum("rk,kci->cri", onehot, contrib, precision=lax.Precision.HIGHEST)
    partial_rows = summed.reshape(vector_count, row_tiles * tile_size)
    rows_piece = lax.psum_scatter(partial_rows, "col", scatter_dimension=1, tiled=True)
    total_rows = rows_dev * lax.axis_size("row") * lax.axis_size("col")
    gram_local = (
        jnp.dot(
            rows_piece,
            rows_piece.T,
            precision=lax.Precision.HIGHEST,
            preferred_element_type=jnp.float32,
        )
        / total_rows
    )
    lower_factor = jnp.linalg.cholesky(lax.psum(gram_local, ("row", "col")))
    basis = jax.scipy.linalg.solve_triangular(lower_factor, rows_piece, lower=True)
    return (basis, lower_factor.T)


def solution(mesh):
    placed = (
        P(None, ("col", "row")),
        P(("row", "col"), None, None),
        P(("row", "col"), None),
        P(("row", "col")),
    )
    return jax.shard_map(
        local, mesh=mesh, in_specs=placed, out_specs=(P(None, ("row", "col")), P()), check_vma=False
    )
```

profile of v0, /device:TPU:1, one launch (start us, length us, event | category | flops | bytes accessed | tf_op | source)
XLA Modules:
  0.0 378.0 jit_solution(10577570718162683185)
XLA Ops:
  7.2 0.0 copy-start
  7.2 0.0 all-gather.2.cloned.1.call-start
  7.2 0.7 all-gather.2.cloned.1.call-update
  7.9 0.0 reduce-scatter.2.cloned.1.call-start
  8.8 0.8 slice_bitcast_fusion
  9.6 0.7 and_bitcast_fusion
  10.2 93.7 %all-gather.2.cloned.1.call-done = bf16[64,8192]{1,0:T(8,128)(2,1)} async-done(((bf16[64,256]{1,0:T(8,128)(2,1)}), bf16[64,8192]{1,0:T(8,128)(2,1)}) %all-gather.2.cloned.1.call-update) | async-done | bytes 1048592 | tf_op jit(solution)/shard_map/all_gather | solution.py:13
  103.9 2.3 copy.23
  106.3 2.8 gather_fusion
  109.0 0.0 copy-done
  109.0 2.2 fusion.2
  111.2 2.1 fusion
  113.4 2.5 copy.19
  115.9 0.0 reduce-scatter.2.cloned.1.call-update
  115.9 114.9 %reduce-scatter.2.cloned.1.call-done = f32[64,256]{1,0:T(8,128)} async-done(((f32[64,8192]{1,0:T(8,128)}), f32[64,256]{1,0:T(8,128)}) %reduce-scatter.2.cloned.1.call-update) | async-done | bytes 65552 | tf_op jit(solution)/shard_map/reduce_scatter | solution.py:23
  230.9 1.1 convolution_multiply_fusion
  232.0 124.6 %psum.7 = f32[64,64]{0,1:T(8,128)S(1)} all-reduce(f32[64,64]{0,1:T(8,128)S(1)} %convolution_multiply_fusion), channel_id=1, replica_groups=mesh['row'=32,'col'=32] {'row','col'}, use_global_device_ids=true, to_apply=%region_1.2 | all-reduce | flops 4096 | bytes 32768 | tf_op jit(solution)/shard_map/psum | solution.py:34
  356.6 0.1 copy.15
  356.7 5.8 %cholesky.16 = f32[64,64]{1,0:T(8,128)S(1)} custom-call(f32[64,64]{1,0:T(8,128)S(1)} %fusion.9), custom_call_target="Cholesky" | custom-call | tf_op jit(solution)/shard_map/jit(cholesky)/cholesky | solution.py:34
  362.5 0.6 compare_reduce_fusion
  363.2 0.7 fusion.10
  363.8 0.7 copy.16
  364.5 4.9 %custom-call.7 = f32[1,64,64]{1,2,0:T(8,128)S(1)} custom-call(f32[1,64,64]{2,1,0:T(8,128)S(1)} %get-tuple-element.9), custom_call_target="InvertDiagBlocksLowerTriangular" | custom-call | tf_op jit(solution)/shard_map/jit(_solve_triangular)/triangular_solve | solution.py:35
  369.4 1.7 fusion.7
  (4 shorter events, 0.1 us)
Async XLA Ops:
  7.2 101.9 %copy-start = (bf16[24,256,256]{2,1,0:T(8,128)(2,1)S(1)}, bf16[24,256,256]{2,1,0:T(8,128)(2,1)}, u32[]{:S(2)}) copy-start(bf16[24,256,256]{2,1,0:T(8,128)(2,1)} %param.5) | copy-start | bytes 9437188
  7.2 96.7 %all-gather.2.cloned.1.call-start = ((), (), s32[]{:S(2)}) async-start(), calls=%async_computation.1 | async-start | bytes 1081344 | tf_op jit(solution)/shard_map/all_gather | solution.py:13
  7.9 222.9 %reduce-scatter.2.cloned.1.call-start = ((), (), s32[]{:S(2)}) async-start(), calls=%async_computation.2 | async-start | bytes 2162688 | tf_op jit(solution)/shard_map/reduce_scatter | solution.py:23
Sparse Core Ops, SparseCore 0:
  12.2 91.6 all-gather.1
  116.1 114.7 reduce-scatter.1
where the time goes:
time: 378 us
  waiting for transfers between devices  209 us (55%)
  blocking collectives  125 us (33%)
  between operations  14.9 us (4%)
  other arithmetic  13.5 us (4%)
  local copies, waits for them, and re-layouts  8.44 us (2%)
  matrix products  7.19 us (2%)
    psum x1, blocking collectives, local(): lower_factor = jnp.linalg.cholesky(lax.psum(gram_local, ('row', 'col')))  125 us
    reduce_scatter x1, waiting for transfers between devices, local(): lax.psum_scatter(partial_rows, 'col', scatter_dimension=1, tiled=True)  115 us
    all_gather x1, waiting for transfers between devices, local(): gathered = lax.all_gather(x_block, 'row', axis=1, tiled=True)  93.7 us
  transfers between devices with their start and end apart: 2, of which 2 were waited for; matrix products, arithmetic and copies ran while one was open for 0% of the time, Pallas kernels for 0%

commit v1 on v0

v1 whole, which is shorter than its diff:
```python
import functools

import jax
import jax.numpy as jnp
from jax import lax
from jax.experimental import pallas as pl
from jax.experimental.pallas import tpu as pltpu
from jax.sharding import PartitionSpec as P

MESH = pl.DeviceIdType.MESH
HIGH = lax.Precision.HIGHEST
NT = (((1,), (1,)), ((), ()))
DIMS = (4, 8, 16)


def far_first(n):
    return sorted(range(1, n), key=lambda k: -min(k, n - k))


def exchange(
    dims, slots, total, table, x_hbm, tiles_hbm, gram_ref, y_ref,
    blocks, tiles, acc, give, take, ring_out, ring_in, pack, gin, yin, zin, gall, cut,
    local_sem, ay_s, ay_r, ax_s, ax_r, ex_s, ex_r, ring_s, ring_r, g_s, g_r, gy_s, gy_r, gz_s, gz_r, f_s, f_r,
):
    nx, ny, nz = dims
    half = nz // 2
    row, col = lax.axis_index("row"), lax.axis_index("col")
    x, y = row // ny, row % ny
    z, c = col // 2, col % 2
    vecs = y_ref.shape[0]
    part = vecs // 2

    def at(dx=0, dy=0, dz=0, dc=0):
        return (lax.rem(x + dx, nx) * ny + lax.rem(y + dy, ny), lax.rem(z + dz, nz) * 2 + lax.rem(c + dc, 2))

    def copy(src, dst, send, recv, dev):
        return pltpu.make_async_remote_copy(
            src_ref=src, dst_ref=dst, send_sem=send, recv_sem=recv, device_id=dev, device_id_type=MESH
        )

    near = [at(dy=k) for k in range(1, ny)] + [at(dx=k) for k in range(1, nx)]
    near += [at(dc=1), at(dz=1), at(dz=nz - 1)]
    barrier = pltpu.get_barrier_semaphore()
    for dev in near:
        pl.semaphore_signal(barrier, inc=1, device_id=dev, device_id_type=MESH)
    get_x = pltpu.make_async_copy(x_hbm, blocks.at[row], local_sem.at[0])
    get_x.start()
    get_tiles = pltpu.make_async_copy(tiles_hbm, tiles, local_sem.at[1])
    get_tiles.start()
    acc[slots] = jnp.zeros_like(acc[slots])
    get_x.wait()
    pl.semaphore_wait(barrier, len(near))

    def gather_y(k):
        return copy(blocks.at[row], blocks.at[row], ay_s.at[k], ay_r.at[k], at(dy=k))

    def landed_y(k):
        slot = blocks.at[x * ny + lax.rem(y + ny - k, ny)]
        return copy(slot, slot, ay_s.at[k], ay_r.at[k], at(dy=k))

    def gather_x(k, m):
        slot = blocks.at[x * ny + lax.rem(y + ny - k, ny)]
        return copy(slot, slot, ax_s.at[k, m], ax_r.at[k, m], at(dx=m))

    def landed_x(k, m):
        slot = blocks.at[lax.rem(x + nx - m, nx) * ny + lax.rem(y + ny - k, ny)]
        return copy(slot, slot, ax_s.at[k, m], ax_r.at[k, m], at(dx=m))

    for k in far_first(ny):
        gather_y(k).start()
    for m in far_first(nx):
        gather_x(0, m).start()
    for k in reversed(far_first(ny)):
        landed_y(k).wait_recv()
        for m in far_first(nx):
            gather_x(k, m).start()
    for k in [0] + list(reversed(far_first(ny))):
        for m in range(1, nx):
            landed_x(k, m).wait_recv()
    get_tiles.wait()

    def product(g, carry):
        for u in range(4):
            k = g * 4 + u
            acc[k] = lax.dot_general(
                blocks[table[k]], tiles[k], NT, preferred_element_type=jnp.float32
            )
        return carry

    lax.fori_loop(0, slots // 4, product, 0)

    def chain(k, carry):
        acc[k] = acc[k] + acc[table[slots + k]]
        return carry

    lax.fori_loop(0, slots, chain, 0)

    def partial(d, core):
        return acc[table[2 * slots + lax.rem(z + d, nz) * 2 + core]]

    def swap(d):
        return copy(give.at[d], take.at[d], ex_s.at[d], ex_r.at[d], at(dc=1))

    def offset(n):
        return lax.rem(nz + half + jnp.where(n % 2 == 0, n // 2, nz - (n + 1) // 2), nz)

    def hand(n, carry):
        d = offset(n)
        give[d] = partial(d, 1 - c)
        swap(d).start()
        return carry

    lax.fori_loop(0, nz, hand, 0)

    def own(d):
        swap(d).wait_recv()
        return partial(d, c) + take[d]

    top, low = pl.ds(0, part), pl.ds(part, part)

    def hop(way, s, h):
        rows = pl.ds(h * part, part)
        return copy(
            ring_out.at[way, s, rows], ring_in.at[way, s, rows], ring_s.at[way, s, h], ring_r.at[way, s, h],
            at(dz=1 if way == 0 else nz - 1),
        )

    v = own(half)
    ring_out[0, 0, top] = v[:part]
    hop(0, 0, 0).start()
    ring_out[1, 0, low] = v[part:]
    hop(1, 0, 1).start()

    def fill(s, carry):
        ring_out[0, s] = own(half - s)
        ring_out[1, s] = own(half + s)
        return carry

    lax.fori_loop(1, half, fill, 0)
    y_ref[...] = own(0)
    hop(0, 1, 1).start()
    hop(1, 1, 0).start()
    hop(0, 0, 0).wait_recv()
    ring_out[0, 1, top] += ring_in[0, 0, top]
    hop(0, 1, 0).start()
    hop(1, 0, 1).wait_recv()
    ring_out[1, 1, low] += ring_in[1, 0, low]
    hop(1, 1, 1).start()

    def step(s, carry):
        for h in range(2):
            for way in range(2):
                rows = top if (h == 0) == (way == 1) else low
                g = h if way == 1 else 1 - h
                hop(way, s - 1, g).wait_recv()
                ring_out[way, s, rows] += ring_in[way, s - 1, rows]
                hop(way, s, g).start()
        return carry

    lax.fori_loop(2, half, step, 0)
    for way in range(2):
        for h in range(2):
            hop(way, half - 1, h).wait_recv()
    whole = y_ref[...] + ring_in[0, half - 1] + ring_in[1, half - 1]
    y_ref[...] = whole

    gram = lax.dot_general(whole, whole, NT, precision=HIGH, preferred_element_type=jnp.float32) * (1.0 / total)
    wide = jnp.concatenate([gram[:part], gram[part:]], axis=1)
    parts = nx * 2
    rows = part // parts
    mine = x * 2 + c
    for q in range(parts):
        pack[q] = wide[q * rows : (q + 1) * rows]

    around = [(dx, dc) for dx in range(nx) for dc in range(2) if (dx, dc) != (0, 0)]

    def place(dx, dc):
        return lax.rem(x + dx, nx) * 2 + lax.rem(c + dc, 2)

    def spread(dx, dc):
        n = dx * 2 + dc
        return copy(pack.at[place(dx, dc)], gin.at[mine], g_s.at[n], g_r.at[n], at(dx=dx, dc=dc))

    for dx, dc in around:
        spread(dx, dc).start()
    gin[mine] = pack[mine]
    for dx, dc in around:
        spread(dx, dc).wait_recv()
    s = gin[0]
    for q in range(1, parts):
        s = s + gin[q]
    yin[y] = s

    def over_y(k):
        return copy(yin.at[y], yin.at[y], gy_s.at[k], gy_r.at[k], at(dy=k))

    for k in far_first(ny):
        over_y(k).start()
    for k in range(1, ny):
        slot = yin.at[lax.rem(y + ny - k, ny)]
        copy(slot, slot, gy_s.at[k], gy_r.at[k], at(dy=k)).wait_recv()
    s = yin[0]
    for q in range(1, ny):
        s = s + yin[q]
    zin[z] = s

    def over_z(k):
        return copy(zin.at[z], zin.at[z], gz_s.at[k], gz_r.at[k], at(dz=k))

    for k in far_first(nz):
        over_z(k).start()
    for k in range(1, nz):
        slot = zin.at[lax.rem(z + nz - k, nz)]
        copy(slot, slot, gz_s.at[k], gz_r.at[k], at(dz=k)).wait_recv()
    s = zin[0]
    for q in range(1, nz):
        s = s + zin[q]
    gall[mine] = s

    def collect(dx, dc):
        n = dx * 2 + dc
        return copy(gall.at[mine], gall.at[mine], f_s.at[n], f_r.at[n], at(dx=dx, dc=dc))

    for dx, dc in around:
        collect(dx, dc).start()
    for dx, dc in around:
        n = dx * 2 + dc
        slot = gall.at[lax.rem(x + nx - dx, nx) * 2 + lax.rem(c + dc, 2)]
        copy(slot, slot, f_s.at[n], f_r.at[n], at(dx=dx, dc=dc)).wait_recv()
    for q in range(parts):
        gram_ref[q * rows : (q + 1) * rows] = gall[q]

    for k in range(1, ny):
        gather_y(k).wait_send()
        over_y(k).wait_send()
    for k in range(ny):
        for m in range(1, nx):
            gather_x(k, m).wait_send()
    for k in range(1, nz):
        over_z(k).wait_send()
    for dx, dc in around:
        spread(dx, dc).wait_send()
        collect(dx, dc).wait_send()

    def drain(d, carry):
        swap(d).wait_send()
        return carry

    lax.fori_loop(0, nz, drain, 0)
    hop(0, 0, 0).wait_send()
    hop(1, 0, 1).wait_send()

    def drain_ring(s, carry):
        for way in range(2):
            for h in range(2):
                hop(way, s, h).wait_send()
        return carry

    lax.fori_loop(1, half, drain_ring, 0)


def orthonormal(gram_ref, y_ref, basis_ref, factor_ref):
    n = y_ref.shape[0]
    half = n // 2
    packed = gram_ref[...]
    gram = jnp.concatenate([packed[:, :n], packed[:, n:]], axis=0)
    lane = lax.broadcasted_iota(jnp.int32, (n, n), 1)
    line = lax.broadcasted_iota(jnp.int32, (n, n), 0)
    work = jnp.concatenate([gram, (lane == line).astype(jnp.float32)], axis=1)
    groups = [work[g * 8 : (g + 1) * 8] for g in range(n // 8)]
    sub = lax.broadcasted_iota(jnp.int32, (8, 1), 0)
    for k in range(n):
        g, r = k // 8, k % 8
        pivot_row = groups[g][r : r + 1]
        scaled = pivot_row / pivot_row[:, k : k + 1]
        for i in range(g, n // 8):
            column = groups[i][:, k : k + 1]
            if i == g:
                column = jnp.where(sub > r, column, 0.0)
            groups[i] = groups[i] - column * scaled
    done = jnp.concatenate(groups, axis=0)
    diag = jnp.sum(jnp.where(lane == line, done[:, :n], 0.0), axis=1, keepdims=True)
    done = done / jnp.sqrt(diag)
    factor_ref[...] = jnp.where(lane >= line, done[:, :n], 0.0)
    basis_ref[...] = jnp.dot(done[:, n:], y_ref[...], precision=HIGH, preferred_element_type=jnp.float32)


def local(dims, x_block, tiles, coords, counts):
    nx, ny, nz = dims
    vecs, width = x_block.shape
    slots = tiles.shape[0]
    lines = 2 * nz
    half = nz // 2
    parts = nx * 2
    rows = vecs // 2 // parts
    total = width * nx * ny * nz * 2
    order = jnp.arange(slots, dtype=jnp.int32)
    live = order < counts[0]
    wanted = jnp.concatenate([coords[:, 0], jnp.arange(lines, dtype=jnp.int32)])
    limit = jnp.concatenate([order, jnp.full((lines,), slots, jnp.int32)])
    hit = (wanted[:, None] == coords[:, 0][None, :]) & live[None, :] & (order[None, :] < limit[:, None])
    last = jnp.max(jnp.where(hit, order[None, :], -1), axis=1)
    table = jnp.concatenate([coords[:, 1], jnp.where(last < 0, slots, last)])
    dma = pltpu.SemaphoreType.DMA
    f32 = jnp.float32
    gram, y = pl.pallas_call(
        functools.partial(exchange, dims, slots, total),
        name="exchange",
        out_shape=(jax.ShapeDtypeStruct((vecs // 2, 2 * vecs), f32), jax.ShapeDtypeStruct((vecs, width), f32)),
        in_specs=[
            pl.BlockSpec(memory_space=pltpu.SMEM),
            pl.BlockSpec(memory_space=pl.ANY),
            pl.BlockSpec(memory_space=pl.ANY),
        ],
        out_specs=(pl.BlockSpec(memory_space=pltpu.VMEM), pl.BlockSpec(memory_space=pltpu.VMEM)),
        scratch_shapes=[
            pltpu.VMEM((nx * ny, vecs, width), jnp.bfloat16),
            pltpu.VMEM(tiles.shape, jnp.bfloat16),
            pltpu.VMEM((slots + 1, vecs, width), f32),
            pltpu.VMEM((nz, vecs, width), f32),
            pltpu.VMEM((nz, vecs, width), f32),
            pltpu.VMEM((2, half, vecs, width), f32),
            pltpu.VMEM((2, half, vecs, width), f32),
            pltpu.VMEM((parts, rows, 2 * vecs), f32),
            pltpu.VMEM((parts, rows, 2 * vecs), f32),
            pltpu.VMEM((ny, rows, 2 * vecs), f32),
            pltpu.VMEM((nz, rows, 2 * vecs), f32),
            pltpu.VMEM((parts, rows, 2 * vecs), f32),
            pltpu.VMEM((8, 128), f32),
            dma((2,)),
            dma((ny,)), dma((ny,)),
            dma((ny, nx)), dma((ny, nx)),
            dma((nz,)), dma((nz,)),
            dma((2, half, 2)), dma((2, half, 2)),
            dma((parts,)), dma((parts,)),
            dma((ny,)), dma((ny,)),
            dma((nz,)), dma((nz,)),
            dma((parts,)), dma((parts,)),
        ],
        compiler_params=pltpu.CompilerParams(
            collective_id=0, has_side_effects=True, vmem_limit_bytes=48 * 1024 * 1024
        ),
    )(table, x_block, tiles)
    return pl.pallas_call(
        orthonormal,
        name="orthonormal",
        out_shape=(jax.ShapeDtypeStruct((vecs, width), f32), jax.ShapeDtypeStruct((vecs, vecs), f32)),
        in_specs=[pl.BlockSpec(memory_space=pltpu.VMEM)] * 2,
        out_specs=(pl.BlockSpec(memory_space=pltpu.VMEM), pl.BlockSpec(memory_space=pltpu.VMEM)),
    )(gram, y)


def solution(mesh):
    placed = (
        P(None, ("col", "row")),
        P(("row", "col"), None, None),
        P(("row", "col"), None),
        P(("row", "col")),
    )
    return jax.shard_map(
        functools.partial(local, DIMS),
        mesh=mesh,
        in_specs=placed,
        out_specs=(P(None, ("row", "col")), P()),
        check_vma=False,
    )
```

time: 378 us -> 106 us (0.28)
  waiting for transfers between devices: 209 us -> 0 us
  blocking collectives: 125 us -> 0 us
  Pallas kernels: 0 us -> 98.8 us
  between operations: 14.9 us -> 1.31 us
  other arithmetic: 13.5 us -> 0.91 us
  matrix products: 7.19 us -> 0 us
  local copies, waits for them, and re-layouts: 8.44 us -> 4.61 us
    psum x1 -> x0, blocking collectives: 125 us -> none  [local(): lower_factor = jnp.linalg.cholesky(lax.psum(gram_local, ('row', 'col')))]
    reduce_scatter x1 -> x0, waiting for transfers between devices: 115 us -> none  [local(): lax.psum_scatter(partial_rows, 'col', scatter_dimension=1, tiled=True)]
    pallas_call x0 -> x2, Pallas kernels: none -> 98.8 us  [the longest x1 91.6 us: local(): pl.pallas_call(functools.partial(exchange, dims, slots, total), name='exc...]
    all_gather x1 -> x0, waiting for transfers between devices: 93.7 us -> none  [local(): gathered = lax.all_gather(x_block, 'row', axis=1, tiled=True)]
    another operation x4 -> x0, other arithmetic: 11.4 us -> none  [the longest x3 6.52 us: local(): lower_factor = jnp.linalg.cholesky(lax.psum(gram_local, ('row', 'col')))]
    dot_general x3 -> x0, matrix products: 5.45 us -> none  [the longest x1 2.2 us: local(): jnp.einsum('ckj,kij->kci', picked, tiles, preferred_element_type=jnp.floa...]
  transfers between devices with their start and end apart: 2 -> 0, of which waited for: 2 -> 0; matrix products, arithmetic and copies ran while one was open for 0% -> 0% of each run, Pallas kernels for 0% -> 0%
where the time goes in v1:
time: 106 us
  Pallas kernels  98.8 us (93%)
  local copies, waits for them, and re-layouts  4.61 us (4%)
  between operations  1.31 us (1%)
    pallas_call x1, Pallas kernels, local(): pl.pallas_call(functools.partial(exchange, dims, slots, total), name='exc...  91.6 us
    pallas_call x1, Pallas kernels, local(): pl.pallas_call(orthonormal, name='orthonormal', out_shape=(jax.ShapeDtype...  7.2 us
    unnamed x8, local copies, waits for them, and re-layouts  3.85 us

profile of v1, /device:TPU:1, one launch (start us, length us, event | category | flops | bytes accessed | tf_op | source)
XLA Modules:
  0.0 105.6 jit_solution(10661499839774246488)
XLA Ops:
  1.3 0.8 slice_bitcast_fusion.1
  2.1 0.1 pad_add_fusion
  2.1 0.7 select_reduce_fusion
  2.9 0.1 pad_add_fusion.1.table
  3.0 0.0 copy-start
  3.0 1.9 %copy-done = bf16[24,256,256]{2,1,0:T(8,128)(2,1)S(1)} copy-done((bf16[24,256,256]{2,1,0:T(8,128)(2,1)S(1)}, bf16[24,256,256]{2,1,0:T(8,128)(2,1)}, u32[]{:S(2)}) %copy-start) | copy-done | bytes 3145752
  4.9 0.0 copy-start.2
  4.9 0.8 copy-done.2
  5.6 91.6 %exchange.1 = (f32[32,128]{1,0:T(8,128)S(1)}, f32[64,256]{1,0:T(8,128)S(1)}) custom-call(s32[80]{0:T(128)S(1)} %pad_add_fusion.1.table, bf16[64,256]{1,0:T(8,128)(2,1)S(1)} %copy-done.2, bf16[24,256,256]{2,1,0:T(8,128)(2,1)S(1)} %copy-done), custom_call_target="tpu_custom_call" | custom-call | tf_op jit(solution)/shard_map/exchange/pallas_call | solution.py:306
  97.2 0.0 copy-start.1
  97.2 0.6 copy-done.1
  97.8 0.0 copy-start.3
  97.8 0.6 copy-done.3
  98.4 7.2 %orthonormal.1 = (f32[64,256]{1,0:T(8,128)}, f32[64,64]{1,0:T(8,128)}) custom-call(f32[32,128]{1,0:T(8,128)} %copy-done.3, f32[64,256]{1,0:T(8,128)} %copy-done.1), custom_call_target="tpu_custom_call" | custom-call | tf_op jit(solution)/shard_map/orthonormal/pallas_call | solution.py:344
  (3 shorter events, 0.0 us)
Async XLA Ops:
  3.0 1.9 %copy-start = (bf16[24,256,256]{2,1,0:T(8,128)(2,1)S(1)}, bf16[24,256,256]{2,1,0:T(8,128)(2,1)}, u32[]{:S(2)}) copy-start(bf16[24,256,256]{2,1,0:T(8,128)(2,1)} %tiles_hbm.1) | copy-start | bytes 9437188
  4.9 0.8 copy-start.2
  97.2 0.6 copy-start.1
  97.8 0.6 copy-start.3

commit v2 on v1

--- a/solution.py
+++ b/solution.py
@@ -13,13 +13,21 @@
 DIMS = (4, 8, 16)
 
 
+NEAR = 3
+CHUNKS = 4
+
+
+def near_first(n):
+    return sorted(range(1, n), key=lambda k: min(k, n - k))
+
+
 def far_first(n):
-    return sorted(range(1, n), key=lambda k: -min(k, n - k))
+    return near_first(n)[::-1]
 
 
 def exchange(
-    dims, slots, total, table, x_hbm, tiles_hbm, gram_ref, y_ref,
-    blocks, tiles, acc, give, take, ring_out, ring_in, pack, gin, yin, zin, gall, cut,
+    dims, slots, total, coords, counts, x_hbm, tiles_hbm, gram_ref, y_ref,
+    table, blocks, tiles, acc, give, take, ring_out, ring_in, pack, gin, yin, zin, gall,
     local_sem, ay_s, ay_r, ax_s, ax_r, ex_s, ex_r, ring_s, ring_r, g_s, g_r, gy_s, gy_r, gz_s, gz_r, f_s, f_r,
 ):
     nx, ny, nz = dims
@@ -38,10 +46,11 @@
             src_ref=src, dst_ref=dst, send_sem=send, recv_sem=recv, device_id=dev, device_id_type=MESH
         )
 
-    near = [at(dy=k) for k in range(1, ny)] + [at(dx=k) for k in range(1, nx)]
-    near += [at(dc=1), at(dz=1), at(dz=nz - 1)]
+    near = max(0, min(NEAR, half - 2))
+    peers = [at(dy=k) for k in range(1, ny)] + [at(dx=k) for k in range(1, nx)] + [at(dc=1)]
+    peers += [at(dz=k) for k in sorted({1, near + 1, nz - near - 1, nz - 1})]
     barrier = pltpu.get_barrier_semaphore()
-    for dev in near:
+    for dev in peers:
         pl.semaphore_signal(barrier, inc=1, device_id=dev, device_id_type=MESH)
     get_x = pltpu.make_async_copy(x_hbm, blocks.at[row], local_sem.at[0])
     get_x.start()
@@ -49,7 +58,7 @@
     get_tiles.start()
     acc[slots] = jnp.zeros_like(acc[slots])
     get_x.wait()
-    pl.semaphore_wait(barrier, len(near))
+    pl.semaphore_wait(barrier, len(peers))
 
     def gather_y(k):
         return copy(blocks.at[row], blocks.at[row], ay_s.at[k], ay_r.at[k], at(dy=k))
@@ -58,25 +67,74 @@
         slot = blocks.at[x * ny + lax.rem(y + ny - k, ny)]
         return copy(slot, slot, ay_s.at[k], ay_r.at[k], at(dy=k))
 
+    beside = sorted({1, nx - 1})
+
+    def slot_of(dx, k):
+        return blocks.at[lax.rem(x + nx - dx, nx) * ny + lax.rem(y + ny - k, ny)]
+
     def gather_x(k, m):
-        slot = blocks.at[x * ny + lax.rem(y + ny - k, ny)]
+        slot = slot_of(0, k)
         return copy(slot, slot, ax_s.at[k, m], ax_r.at[k, m], at(dx=m))
 
     def landed_x(k, m):
-        slot = blocks.at[lax.rem(x + nx - m, nx) * ny + lax.rem(y + ny - k, ny)]
+        slot = slot_of(m, k)
         return copy(slot, slot, ax_s.at[k, m], ax_r.at[k, m], at(dx=m))
 
-    for k in far_first(ny):
+    def passed(k):
+        return nx == 4 and min(k, ny - k) <= 2
+
+    def relays(k, m):
+        return passed(k) and m == (1 if k % 2 == 0 else 3)
+
+    def pass_x(k):
+        m = 1 if k % 2 == 0 else 3
+        slot = slot_of(m, k)
+        return copy(slot, slot, ax_s.at[k, 2], ax_r.at[k, 2], at(dx=m))
+
+    def relay_x(k):
+        if passed(k):
+            landed_x(k, 1 if k % 2 == 0 else 3).wait_recv()
+            pass_x(k).start()
+
+    for k in near_first(ny):
         gather_y(k).start()
-    for m in far_first(nx):
+    for m in beside:
         gather_x(0, m).start()
-    for k in reversed(far_first(ny)):
+
+    used = counts[0]
+    lines = [coords[0, k] for k in range(slots)]
+
+    def latest(line, below):
+        found = jnp.int32(slots)
+        for k in range(slots):
+            found = jnp.where((lines[k] == line) & (k < below), k, found)
+        return found
+
+    def link(k, carry):
+        table[k] = coords[1, k]
+        table[slots + k] = latest(coords[0, k], k)
+        return carry
+
+    lax.fori_loop(0, slots, link, 0)
+
+    def ends(r, carry):
+        table[2 * slots + r] = latest(r, used)
+        return carry
+
+    lax.fori_loop(0, 2 * nz, ends, 0)
+
+    for k in near_first(ny):
         landed_y(k).wait_recv()
-        for m in far_first(nx):
+        for m in beside if passed(k) or nx != 4 else [2] + beside:
             gather_x(k, m).start()
-    for k in [0] + list(reversed(far_first(ny))):
+        if k == 1:
+            relay_x(0)
+    for k in near_first(ny):
+        relay_x(k)
+    for k in [0] + near_first(ny):
         for m in range(1, nx):
-            landed_x(k, m).wait_recv()
+            if m not in beside or not relays(k, m):
+                landed_x(k, m).wait_recv()
     get_tiles.wait()
 
     def product(g, carry):
@@ -98,70 +156,72 @@
     def partial(d, core):
         return acc[table[2 * slots + lax.rem(z + d, nz) * 2 + core]]
 
+    stages = []
+    for n in range(half):
+        stages += [d for d in (half - n, near - n) if (d > near and d == half - n) or (0 < d <= near and d == near - n)]
+    order = []
+    for d in stages:
+        order += [d] if d == half else [d, 2 * half - d]
+    order += [0]
+
     def swap(d):
         return copy(give.at[d], take.at[d], ex_s.at[d], ex_r.at[d], at(dc=1))
 
-    def offset(n):
-        return lax.rem(nz + half + jnp.where(n % 2 == 0, n // 2, nz - (n + 1) // 2), nz)
-
-    def hand(n, carry):
-        d = offset(n)
+    for d in order:
         give[d] = partial(d, 1 - c)
         swap(d).start()
-        return carry
-
-    lax.fori_loop(0, nz, hand, 0)
 
     def own(d):
         swap(d).wait_recv()
         return partial(d, c) + take[d]
 
-    top, low = pl.ds(0, part), pl.ds(part, part)
-
-    def hop(way, s, h):
-        rows = pl.ds(h * part, part)
+    size = vecs // CHUNKS
+
+    def hop(way, d, h):
+        rows = pl.ds(h * size, size)
+        dz = near + 1 if d == near + 1 else 1
         return copy(
-            ring_out.at[way, s, rows], ring_in.at[way, s, rows], ring_s.at[way, s, h], ring_r.at[way, s, h],
-            at(dz=1 if way == 0 else nz - 1),
+            ring_out.at[way, d - 1, rows], ring_in.at[way, d - 1, rows], ring_s.at[way, d - 1, h],
+            ring_r.at[way, d - 1, h], at(dz=dz if way == 0 else nz - dz),
         )
 
-    v = own(half)
-    ring_out[0, 0, top] = v[:part]
-    hop(0, 0, 0).start()
-    ring_out[1, 0, low] = v[part:]
-    hop(1, 0, 1).start()
-
-    def fill(s, carry):
-        ring_out[0, s] = own(half - s)
-        ring_out[1, s] = own(half + s)
-        return carry
-
-    lax.fori_loop(1, half, fill, 0)
+    def fresh(way, d):
+        if d == half:
+            return [h for h in range(CHUNKS) if (h < CHUNKS // 2) == (way == 0)]
+        if d == half - 1:
+            return [h for h in range(CHUNKS) if (h < CHUNKS // 2) != (way == 0)]
+        return list(range(CHUNKS)) if d == near else []
+
+    def carried(way, d):
+        return [] if d == half else [h for h in range(CHUNKS) if h not in fresh(way, d)]
+
+    for d in stages:
+        if d == half:
+            v = own(d)
+            ring_out[0, d - 1, :part] = v[:part]
+            ring_out[1, d - 1, part:] = v[part:]
+        else:
+            ring_out[0, d - 1] = own(d)
+            ring_out[1, d - 1] = own(2 * half - d)
+        for way in range(2):
+            for h in fresh(way, d):
+                hop(way, d, h).start()
     y_ref[...] = own(0)
-    hop(0, 1, 1).start()
-    hop(1, 1, 0).start()
-    hop(0, 0, 0).wait_recv()
-    ring_out[0, 1, top] += ring_in[0, 0, top]
-    hop(0, 1, 0).start()
-    hop(1, 0, 1).wait_recv()
-    ring_out[1, 1, low] += ring_in[1, 0, low]
-    hop(1, 1, 1).start()
-
-    def step(s, carry):
-        for h in range(2):
+    for d in stages:
+        for h in range(CHUNKS):
             for way in range(2):
-                rows = top if (h == 0) == (way == 1) else low
-                g = h if way == 1 else 1 - h
-                hop(way, s - 1, g).wait_recv()
-                ring_out[way, s, rows] += ring_in[way, s - 1, rows]
-                hop(way, s, g).start()
-        return carry
-
-    lax.fori_loop(2, half, step, 0)
-    for way in range(2):
-        for h in range(2):
-            hop(way, half - 1, h).wait_recv()
-    whole = y_ref[...] + ring_in[0, half - 1] + ring_in[1, half - 1]
+                if h in carried(way, d):
+                    rows = pl.ds(h * size, size)
+                    hop(way, d + 1, h).wait_recv()
+                    ring_out[way, d - 1, rows] += ring_in[way, d, rows]
+                    hop(way, d, h).start()
+    for d in sorted({near + 1, 1}):
+        for way in range(2):
+            for h in range(CHUNKS):
+                hop(way, d, h).wait_recv()
+    whole = y_ref[...] + ring_in[0, 0] + ring_in[1, 0]
+    if near > 0:
+        whole = whole + ring_in[0, near] + ring_in[1, near]
     y_ref[...] = whole
 
     gram = lax.dot_general(whole, whole, NT, precision=HIGH, preferred_element_type=jnp.float32) * (1.0 / total)
@@ -234,33 +294,28 @@
         gather_y(k).wait_send()
         over_y(k).wait_send()
     for k in range(ny):
-        for m in range(1, nx):
+        for m in beside:
             gather_x(k, m).wait_send()
+        if nx == 4:
+            pass_x(k).wait_send()
     for k in range(1, nz):
         over_z(k).wait_send()
     for dx, dc in around:
         spread(dx, dc).wait_send()
         collect(dx, dc).wait_send()
 
-    def drain(d, carry):
+    for d in order:
         swap(d).wait_send()
-        return carry
-
-    lax.fori_loop(0, nz, drain, 0)
-    hop(0, 0, 0).wait_send()
-    hop(1, 0, 1).wait_send()
-
-    def drain_ring(s, carry):
+    for d in stages:
         for way in range(2):
-            for h in range(2):
-                hop(way, s, h).wait_send()
-        return carry
-
-    lax.fori_loop(1, half, drain_ring, 0)
-
-
-def orthonormal(gram_ref, y_ref, basis_ref, factor_ref):
+            for h in fresh(way, d) + carried(way, d):
+                hop(way, d, h).wait_send()
+
+
+def orthonormal(gram_ref, y_hbm, basis_ref, factor_ref, y_ref, y_sem):
     n = y_ref.shape[0]
+    get_y = pltpu.make_async_copy(y_hbm, y_ref, y_sem)
+    get_y.start()
     half = n // 2
     packed = gram_ref[...]
     gram = jnp.concatenate([packed[:, :n], packed[:, n:]], axis=0)
@@ -282,6 +337,7 @@
     diag = jnp.sum(jnp.where(lane == line, done[:, :n], 0.0), axis=1, keepdims=True)
     done = done / jnp.sqrt(diag)
     factor_ref[...] = jnp.where(lane >= line, done[:, :n], 0.0)
+    get_y.wait()
     basis_ref[...] = jnp.dot(done[:, n:], y_ref[...], precision=HIGH, preferred_element_type=jnp.float32)
 
 
@@ -289,18 +345,10 @@
     nx, ny, nz = dims
     vecs, width = x_block.shape
     slots = tiles.shape[0]
-    lines = 2 * nz
     half = nz // 2
     parts = nx * 2
     rows = vecs // 2 // parts
     total = width * nx * ny * nz * 2
-    order = jnp.arange(slots, dtype=jnp.int32)
-    live = order < counts[0]
-    wanted = jnp.concatenate([coords[:, 0], jnp.arange(lines, dtype=jnp.int32)])
-    limit = jnp.concatenate([order, jnp.full((lines,), slots, jnp.int32)])
-    hit = (wanted[:, None] == coords[:, 0][None, :]) & live[None, :] & (order[None, :] < limit[:, None])
-    last = jnp.max(jnp.where(hit, order[None, :], -1), axis=1)
-    table = jnp.concatenate([coords[:, 1], jnp.where(last < 0, slots, last)])
     dma = pltpu.SemaphoreType.DMA
     f32 = jnp.float32
     gram, y = pl.pallas_call(
@@ -309,11 +357,13 @@
         out_shape=(jax.ShapeDtypeStruct((vecs // 2, 2 * vecs), f32), jax.ShapeDtypeStruct((vecs, width), f32)),
         in_specs=[
             pl.BlockSpec(memory_space=pltpu.SMEM),
-            pl.BlockSpec(memory_space=pl.ANY),
-            pl.BlockSpec(memory_space=pl.ANY),
+            pl.BlockSpec(memory_space=pltpu.SMEM),
+            pl.BlockSpec(memory_space=pltpu.HBM),
+            pl.BlockSpec(memory_space=pltpu.HBM),
         ],
         out_specs=(pl.BlockSpec(memory_space=pltpu.VMEM), pl.BlockSpec(memory_space=pltpu.VMEM)),
         scratch_shapes=[
+            pltpu.SMEM((2 * slots + 2 * nz,), jnp.int32),
             pltpu.VMEM((nx * ny, vecs, width), jnp.bfloat16),
             pltpu.VMEM(tiles.shape, jnp.bfloat16),
             pltpu.VMEM((slots + 1, vecs, width), f32),
@@ -326,27 +376,28 @@
             pltpu.VMEM((ny, rows, 2 * vecs), f32),
             pltpu.VMEM((nz, rows, 2 * vecs), f32),
             pltpu.VMEM((parts, rows, 2 * vecs), f32),
-            pltpu.VMEM((8, 128), f32),
             dma((2,)),
             dma((ny,)), dma((ny,)),
             dma((ny, nx)), dma((ny, nx)),
             dma((nz,)), dma((nz,)),
-            dma((2, half, 2)), dma((2, half, 2)),
+            dma((2, half, CHUNKS)), dma((2, half, CHUNKS)),
             dma((parts,)), dma((parts,)),
             dma((ny,)), dma((ny,)),
             dma((nz,)), dma((nz,)),
             dma((parts,)), dma((parts,)),
         ],
         compiler_params=pltpu.CompilerParams(
-            collective_id=0, has_side_effects=True, vmem_limit_bytes=48 * 1024 * 1024
+            collective_id=0, has_side_effects=True, vmem_limit_bytes=62 * 1024 * 1024
         ),
-    )(table, x_block, tiles)
+    )(coords.T, counts, x_block, tiles)
     return pl.pallas_call(
         orthonormal,
         name="orthonormal",
         out_shape=(jax.ShapeDtypeStruct((vecs, width), f32), jax.ShapeDtypeStruct((vecs, vecs), f32)),
-        in_specs=[pl.BlockSpec(memory_space=pltpu.VMEM)] * 2,
+        in_specs=[pl.BlockSpec(memory_space=pltpu.VMEM), pl.BlockSpec(memory_space=pltpu.HBM)],
         out_specs=(pl.BlockSpec(memory_space=pltpu.VMEM), pl.BlockSpec(memory_space=pltpu.VMEM)),
+        scratch_shapes=[pltpu.VMEM((vecs, width), f32), dma(())],
+        compiler_params=pltpu.CompilerParams(vmem_limit_bytes=62 * 1024 * 1024),
     )(gram, y)
 
 

time: 106 us -> 92.2 us (0.87)
  Pallas kernels: 98.8 us -> 90.7 us
  local copies, waits for them, and re-layouts: 4.61 us -> 0 us
    pallas_call x1, Pallas kernels: 91.6 us -> 83.6 us  [local(): pl.pallas_call(functools.partial(exchange, dims, slots, total), name='exc...]
    unnamed x8 -> x0, local copies, waits for them, and re-layouts: 3.85 us -> none
where the time goes in v2:
time: 92.2 us; the launch traced here: 92 us
  Pallas kernels  90.7 us (98%)
  between operations  1.29 us (1%)
    pallas_call x1, Pallas kernels, local(): pl.pallas_call(functools.partial(exchange, dims, slots, total), name='exc...  83.6 us
    pallas_call x1, Pallas kernels, local(): pl.pallas_call(orthonormal, name='orthonormal', out_shape=(jax.ShapeDtype...  7.07 us

profile of v2, /device:TPU:1, one launch (start us, length us, event | category | flops | bytes accessed | tf_op | source)
XLA Modules:
  0.0 92.0 jit_solution(7308055033698573605)
XLA Ops:
  1.3 83.6 %exchange.1 = (f32[32,128]{1,0:T(8,128)}, f32[64,256]{1,0:T(8,128)}) custom-call(s32[2,24]{1,0:T(2,128)} %bitcast.1, s32[1]{0:T(128)S(6)} %copy.6.counts, bf16[64,256]{1,0:T(8,128)(2,1)} %x_hbm.1, bf16[24,256,256]{2,1,0:T(8,128)(2,1)} %tiles_hbm.1), custom_call_target="tpu_custom_call" | custom-call | tf_op jit(solution)/shard_map/exchange/pallas_call | solution.py:354
  84.9 7.1 %orthonormal.1 = (f32[64,256]{1,0:T(8,128)}, f32[64,64]{1,0:T(8,128)}) custom-call(f32[32,128]{1,0:T(8,128)} %get-tuple-element.4.gram_ref, f32[64,256]{1,0:T(8,128)} %get-tuple-element.5.y_hbm), custom_call_target="tpu_custom_call" | custom-call | tf_op jit(solution)/shard_map/orthonormal/pallas_call | solution.py:393

commit v3 on v2

--- a/solution.py
+++ b/solution.py
@@ -68,6 +68,7 @@
         return copy(slot, slot, ay_s.at[k], ay_r.at[k], at(dy=k))
 
     beside = sorted({1, nx - 1})
+    corner = sorted({1, ny - 1})
 
     def slot_of(dx, k):
         return blocks.at[lax.rem(x + nx - dx, nx) * ny + lax.rem(y + ny - k, ny)]
@@ -80,25 +81,32 @@
         slot = slot_of(m, k)
         return copy(slot, slot, ax_s.at[k, m], ax_r.at[k, m], at(dx=m))
 
+    def turn(k, m):
+        slot = slot_of(m, 0)
+        return copy(slot, slot, ax_s.at[k, m], ax_r.at[k, m], at(dy=k))
+
     def passed(k):
-        return nx == 4 and min(k, ny - k) <= 2
+        return nx == 4 and k not in corner and 0 < min(k, ny - k) <= 2
+
+    def way_of(k):
+        return 1 if 2 * k <= ny else nx - 1
 
     def relays(k, m):
-        return passed(k) and m == (1 if k % 2 == 0 else 3)
+        return passed(k) and m == way_of(k)
 
     def pass_x(k):
-        m = 1 if k % 2 == 0 else 3
+        m = way_of(k)
         slot = slot_of(m, k)
         return copy(slot, slot, ax_s.at[k, 2], ax_r.at[k, 2], at(dx=m))
 
     def relay_x(k):
         if passed(k):
-            landed_x(k, 1 if k % 2 == 0 else 3).wait_recv()
+            landed_x(k, way_of(k)).wait_recv()
             pass_x(k).start()
 
     for k in near_first(ny):
         gather_y(k).start()
-    for m in beside:
+    for m in range(1, nx):
         gather_x(0, m).start()
 
     used = counts[0]
@@ -123,17 +131,27 @@
 
     lax.fori_loop(0, 2 * nz, ends, 0)
 
+    def move_on(k):
+        landed_y(k).wait_recv()
+        for m in beside if passed(k) else range(1, nx):
+            gather_x(k, m).start()
+
+    beyond = [k for k in near_first(ny) if k not in corner]
+    for k in beyond[:2]:
+        move_on(k)
+    for m in range(1, nx):
+        landed_x(0, m).wait_recv()
+        for k in corner:
+            turn(k, m).start()
+    for k in beyond[2:]:
+        move_on(k)
+    for k in beyond:
+        relay_x(k)
+    for k in corner:
+        landed_y(k).wait_recv()
     for k in near_first(ny):
-        landed_y(k).wait_recv()
-        for m in beside if passed(k) or nx != 4 else [2] + beside:
-            gather_x(k, m).start()
-        if k == 1:
-            relay_x(0)
-    for k in near_first(ny):
-        relay_x(k)
-    for k in [0] + near_first(ny):
         for m in range(1, nx):
-            if m not in beside or not relays(k, m):
+            if not relays(k, m):
                 landed_x(k, m).wait_recv()
     get_tiles.wait()
 
@@ -294,9 +312,12 @@
         gather_y(k).wait_send()
         over_y(k).wait_send()
     for k in range(ny):
-        for m in beside:
-            gather_x(k, m).wait_send()
-        if nx == 4:
+        for m in range(1, nx):
+            if k in corner:
+                turn(k, m).wait_send()
+            elif m in beside or not passed(k):
+                gather_x(k, m).wait_send()
+        if passed(k):
             pass_x(k).wait_send()
     for k in range(1, nz):
         over_z(k).wait_send()
@@ -316,23 +337,45 @@
     n = y_ref.shape[0]
     get_y = pltpu.make_async_copy(y_hbm, y_ref, y_sem)
     get_y.start()
-    half = n // 2
     packed = gram_ref[...]
     gram = jnp.concatenate([packed[:, :n], packed[:, n:]], axis=0)
     lane = lax.broadcasted_iota(jnp.int32, (n, n), 1)
     line = lax.broadcasted_iota(jnp.int32, (n, n), 0)
     work = jnp.concatenate([gram, (lane == line).astype(jnp.float32)], axis=1)
     groups = [work[g * 8 : (g + 1) * 8] for g in range(n // 8)]
-    sub = lax.broadcasted_iota(jnp.int32, (8, 1), 0)
-    for k in range(n):
-        g, r = k // 8, k % 8
-        pivot_row = groups[g][r : r + 1]
-        scaled = pivot_row / pivot_row[:, k : k + 1]
-        for i in range(g, n // 8):
-            column = groups[i][:, k : k + 1]
-            if i == g:
-                column = jnp.where(sub > r, column, 0.0)
-            groups[i] = groups[i] - column * scaled
+    sub = lax.broadcasted_iota(jnp.int32, (8, 2 * n), 0)
+    full = (8, 2 * n)
+    for g in range(n // 8):
+        first = g * 8
+        block = groups[g]
+        rows = [jnp.broadcast_to(block[r : r + 1], full) for r in range(8)]
+        small = [
+            [jnp.broadcast_to(rows[r][:, first + q : first + q + 1], full) if q >= r else None for q in range(8)]
+            for r in range(8)
+        ]
+        times = [[None] * 8 for _ in range(8)]
+        inverse = []
+        for r in range(8):
+            inverse.append(1.0 / small[r][r])
+            for q in range(r + 1, 8):
+                times[q][r] = small[r][q] * inverse[r]
+            for i in range(r + 1, 8):
+                for q in range(i, 8):
+                    small[i][q] = small[i][q] - times[i][r] * small[r][q]
+                rows[i] = rows[i] - times[i][r] * rows[r]
+        block = rows[0]
+        for r in range(1, 8):
+            block = jnp.where(sub == r, rows[r], block)
+        groups[g] = block
+        scaled = [rows[r] * inverse[r] for r in range(8)]
+        for i in range(g + 1, n // 8):
+            block = groups[i]
+            left = [jnp.broadcast_to(block[:, first + r : first + r + 1], full) for r in range(8)]
+            for r in range(8):
+                block = block - left[r] * scaled[r]
+                for q in range(r + 1, 8):
+                    left[q] = left[q] - left[r] * times[q][r]
+            groups[i] = block
     done = jnp.concatenate(groups, axis=0)
     diag = jnp.sum(jnp.where(lane == line, done[:, :n], 0.0), axis=1, keepdims=True)
     done = done / jnp.sqrt(diag)

time: 92.2 us -> 88.9 us (0.964)
  Pallas kernels: 90.7 us -> 87.3 us
    pallas_call x1, Pallas kernels: 7.07 us -> 4.33 us  [local(): pl.pallas_call(orthonormal, name='orthonormal', out_shape=(jax.ShapeDtype...]
where the time goes in v3:
time: 88.9 us; the launch traced here: 88.6 us
  Pallas kernels  87.3 us (98%)
  between operations  1.29 us (1%)
    pallas_call x1, Pallas kernels, local(): pl.pallas_call(functools.partial(exchange, dims, slots, total), name='exc...  83 us
    pallas_call x1, Pallas kernels, local(): pl.pallas_call(orthonormal, name='orthonormal', out_shape=(jax.ShapeDtype...  4.33 us

profile of v3, /device:TPU:1, one launch (start us, length us, event | category | flops | bytes accessed | tf_op | source)
XLA Modules:
  0.0 88.6 jit_solution(9115693603350637832)
XLA Ops:
  1.3 83.0 %exchange.1 = (f32[32,128]{1,0:T(8,128)}, f32[64,256]{1,0:T(8,128)}) custom-call(s32[2,24]{1,0:T(2,128)} %bitcast.1, s32[1]{0:T(128)S(6)} %copy.6.counts, bf16[64,256]{1,0:T(8,128)(2,1)} %x_hbm.1, bf16[24,256,256]{2,1,0:T(8,128)(2,1)} %tiles_hbm.1), custom_call_target="tpu_custom_call" | custom-call | tf_op jit(solution)/shard_map/exchange/pallas_call | solution.py:397
  84.3 4.3 %orthonormal.1 = (f32[64,256]{1,0:T(8,128)}, f32[64,64]{1,0:T(8,128)}) custom-call(f32[32,128]{1,0:T(8,128)} %get-tuple-element.4.gram_ref, f32[64,256]{1,0:T(8,128)} %get-tuple-element.5.y_hbm), custom_call_target="tpu_custom_call" | custom-call | tf_op jit(solution)/shard_map/orthonormal/pallas_call | solution.py:436

commit v4 on v3

--- a/solution.py
+++ b/solution.py
@@ -14,7 +14,7 @@
 
 
 NEAR = 3
-CHUNKS = 4
+CHUNKS = (2, 1)
 
 
 def near_first(n):
@@ -26,8 +26,8 @@
 
 
 def exchange(
-    dims, slots, total, coords, counts, x_hbm, tiles_hbm, gram_ref, y_ref,
-    table, blocks, tiles, acc, give, take, ring_out, ring_in, pack, gin, yin, zin, gall,
+    dims, slots, total, coords, counts, x_hbm, tiles_hbm, gram_ref, y_hbm,
+    table, y_ref, blocks, tiles, acc, give, take, ring_out, ring_in, pack, gin, yin, zin, gall,
     local_sem, ay_s, ay_r, ax_s, ax_r, ex_s, ex_r, ring_s, ring_r, g_s, g_r, gy_s, gy_r, gz_s, gz_r, f_s, f_r,
 ):
     nx, ny, nz = dims
@@ -38,7 +38,14 @@
     vecs = y_ref.shape[0]
     part = vecs // 2
 
+    known = {}
+
     def at(dx=0, dy=0, dz=0, dc=0):
+        if (dx, dy, dz, dc) not in known:
+            known[dx, dy, dz, dc] = place_of(dx, dy, dz, dc)
+        return known[dx, dy, dz, dc]
+
+    def place_of(dx, dy, dz, dc):
         return (lax.rem(x + dx, nx) * ny + lax.rem(y + dy, ny), lax.rem(z + dz, nz) * 2 + lax.rem(c + dc, 2))
 
     def copy(src, dst, send, recv, dev):
@@ -104,10 +111,11 @@
             landed_x(k, way_of(k)).wait_recv()
             pass_x(k).start()
 
-    for k in near_first(ny):
+    beyond = [k for k in near_first(ny) if k not in corner]
+    for m in far_first(nx):
+        gather_x(0, m).start()
+    for k in beyond + corner:
         gather_y(k).start()
-    for m in range(1, nx):
-        gather_x(0, m).start()
 
     used = counts[0]
     lines = [coords[0, k] for k in range(slots)]
@@ -125,18 +133,11 @@
 
     lax.fori_loop(0, slots, link, 0)
 
-    def ends(r, carry):
-        table[2 * slots + r] = latest(r, used)
-        return carry
-
-    lax.fori_loop(0, 2 * nz, ends, 0)
-
     def move_on(k):
         landed_y(k).wait_recv()
         for m in beside if passed(k) else range(1, nx):
             gather_x(k, m).start()
 
-    beyond = [k for k in near_first(ny) if k not in corner]
     for k in beyond[:2]:
         move_on(k)
     for m in range(1, nx):
@@ -145,6 +146,13 @@
             turn(k, m).start()
     for k in beyond[2:]:
         move_on(k)
+
+    def ends(r, carry):
+        table[2 * slots + r] = latest(r, used)
+        return carry
+
+    lax.fori_loop(0, 2 * nz, ends, 0)
+
     for k in beyond:
         relay_x(k)
     for k in corner:
@@ -165,18 +173,21 @@
 
     lax.fori_loop(0, slots // 4, product, 0)
 
-    def chain(k, carry):
-        acc[k] = acc[k] + acc[table[slots + k]]
+    def chain(g, carry):
+        for u in range(4):
+            k = g * 4 + u
+            acc[k] = acc[k] + acc[table[slots + k]]
         return carry
 
-    lax.fori_loop(0, slots, chain, 0)
+    lax.fori_loop(0, slots // 4, chain, 0)
 
     def partial(d, core):
         return acc[table[2 * slots + lax.rem(z + d, nz) * 2 + core]]
 
-    stages = []
-    for n in range(half):
-        stages += [d for d in (half - n, near - n) if (d > near and d == half - n) or (0 < d <= near and d == near - n)]
+    far = list(range(half, near, -1))
+    stages = far[:2]
+    for n in range(max(len(far) - 2, near)):
+        stages += [near - n] * (n < near) + far[n + 2 : n + 3]
     order = []
     for d in stages:
         order += [d] if d == half else [d, 2 * half - d]
@@ -193,25 +204,30 @@
         swap(d).wait_recv()
         return partial(d, c) + take[d]
 
-    size = vecs // CHUNKS
+    def count(d):
+        return CHUNKS[0 if d > near else 1]
+
+    def lines_of(d, h):
+        size = vecs // count(d)
+        return pl.ds(h * size, size)
 
     def hop(way, d, h):
-        rows = pl.ds(h * size, size)
         dz = near + 1 if d == near + 1 else 1
         return copy(
-            ring_out.at[way, d - 1, rows], ring_in.at[way, d - 1, rows], ring_s.at[way, d - 1, h],
+            ring_out.at[way, d - 1, lines_of(d, h)], ring_in.at[way, d - 1, lines_of(d, h)], ring_s.at[way, d - 1, h],
             ring_r.at[way, d - 1, h], at(dz=dz if way == 0 else nz - dz),
         )
 
     def fresh(way, d):
+        every = range(count(d))
         if d == half:
-            return [h for h in range(CHUNKS) if (h < CHUNKS // 2) == (way == 0)]
+            return [h for h in every if (h < count(d) // 2) == (way == 0)]
         if d == half - 1:
-            return [h for h in range(CHUNKS) if (h < CHUNKS // 2) != (way == 0)]
-        return list(range(CHUNKS)) if d == near else []
+            return [h for h in every if (h < count(d) // 2) != (way == 0)]
+        return list(every) if d == near else []
 
     def carried(way, d):
-        return [] if d == half else [h for h in range(CHUNKS) if h not in fresh(way, d)]
+        return [] if d == half else [h for h in range(count(d)) if h not in fresh(way, d)]
 
     for d in stages:
         if d == half:
@@ -226,21 +242,23 @@
                 hop(way, d, h).start()
     y_ref[...] = own(0)
     for d in stages:
-        for h in range(CHUNKS):
+        for h in range(count(d)):
             for way in range(2):
                 if h in carried(way, d):
-                    rows = pl.ds(h * size, size)
+                    rows = lines_of(d, h)
                     hop(way, d + 1, h).wait_recv()
                     ring_out[way, d - 1, rows] += ring_in[way, d, rows]
                     hop(way, d, h).start()
     for d in sorted({near + 1, 1}):
         for way in range(2):
-            for h in range(CHUNKS):
+            for h in range(count(d)):
                 hop(way, d, h).wait_recv()
     whole = y_ref[...] + ring_in[0, 0] + ring_in[1, 0]
     if near > 0:
         whole = whole + ring_in[0, near] + ring_in[1, near]
     y_ref[...] = whole
+    put_y = pltpu.make_async_copy(y_ref, y_hbm, local_sem.at[0])
+    put_y.start()
 
     gram = lax.dot_general(whole, whole, NT, precision=HIGH, preferred_element_type=jnp.float32) * (1.0 / total)
     wide = jnp.concatenate([gram[:part], gram[part:]], axis=1)
@@ -287,27 +305,6 @@
 
     for k in far_first(nz):
         over_z(k).start()
-    for k in range(1, nz):
-        slot = zin.at[lax.rem(z + nz - k, nz)]
-        copy(slot, slot, gz_s.at[k], gz_r.at[k], at(dz=k)).wait_recv()
-    s = zin[0]
-    for q in range(1, nz):
-        s = s + zin[q]
-    gall[mine] = s
-
-    def collect(dx, dc):
-        n = dx * 2 + dc
-        return copy(gall.at[mine], gall.at[mine], f_s.at[n], f_r.at[n], at(dx=dx, dc=dc))
-
-    for dx, dc in around:
-        collect(dx, dc).start()
-    for dx, dc in around:
-        n = dx * 2 + dc
-        slot = gall.at[lax.rem(x + nx - dx, nx) * 2 + lax.rem(c + dc, 2)]
-        copy(slot, slot, f_s.at[n], f_r.at[n], at(dx=dx, dc=dc)).wait_recv()
-    for q in range(parts):
-        gram_ref[q * rows : (q + 1) * rows] = gall[q]
-
     for k in range(1, ny):
         gather_y(k).wait_send()
         over_y(k).wait_send()
@@ -319,18 +316,40 @@
                 gather_x(k, m).wait_send()
         if passed(k):
             pass_x(k).wait_send()
-    for k in range(1, nz):
-        over_z(k).wait_send()
     for dx, dc in around:
         spread(dx, dc).wait_send()
-        collect(dx, dc).wait_send()
-
     for d in order:
         swap(d).wait_send()
     for d in stages:
         for way in range(2):
             for h in fresh(way, d) + carried(way, d):
                 hop(way, d, h).wait_send()
+    for k in range(1, nz):
+        slot = zin.at[lax.rem(z + nz - k, nz)]
+        copy(slot, slot, gz_s.at[k], gz_r.at[k], at(dz=k)).wait_recv()
+    s = zin[0]
+    for q in range(1, nz):
+        s = s + zin[q]
+    gall[mine] = s
+
+    def collect(dx, dc):
+        n = dx * 2 + dc
+        return copy(gall.at[mine], gall.at[mine], f_s.at[n], f_r.at[n], at(dx=dx, dc=dc))
+
+    for dx, dc in around:
+        collect(dx, dc).start()
+    for dx, dc in around:
+        n = dx * 2 + dc
+        slot = gall.at[lax.rem(x + nx - dx, nx) * 2 + lax.rem(c + dc, 2)]
+        copy(slot, slot, f_s.at[n], f_r.at[n], at(dx=dx, dc=dc)).wait_recv()
+    for q in range(parts):
+        gram_ref[q * rows : (q + 1) * rows] = gall[q]
+
+    for k in range(1, nz):
+        over_z(k).wait_send()
+    for dx, dc in around:
+        collect(dx, dc).wait_send()
+    put_y.wait()
 
 
 def orthonormal(gram_ref, y_hbm, basis_ref, factor_ref, y_ref, y_sem):
@@ -404,9 +423,10 @@
             pl.BlockSpec(memory_space=pltpu.HBM),
             pl.BlockSpec(memory_space=pltpu.HBM),
         ],
-        out_specs=(pl.BlockSpec(memory_space=pltpu.VMEM), pl.BlockSpec(memory_space=pltpu.VMEM)),
+        out_specs=(pl.BlockSpec(memory_space=pltpu.VMEM), pl.BlockSpec(memory_space=pltpu.HBM)),
         scratch_shapes=[
             pltpu.SMEM((2 * slots + 2 * nz,), jnp.int32),
+            pltpu.VMEM((vecs, width), f32),
             pltpu.VMEM((nx * ny, vecs, width), jnp.bfloat16),
             pltpu.VMEM(tiles.shape, jnp.bfloat16),
             pltpu.VMEM((slots + 1, vecs, width), f32),
@@ -423,7 +443,7 @@
             dma((ny,)), dma((ny,)),
             dma((ny, nx)), dma((ny, nx)),
             dma((nz,)), dma((nz,)),
-            dma((2, half, CHUNKS)), dma((2, half, CHUNKS)),
+            dma((2, half, max(CHUNKS))), dma((2, half, max(CHUNKS))),
             dma((parts,)), dma((parts,)),
             dma((ny,)), dma((ny,)),
             dma((nz,)), dma((nz,)),

time: 88.9 us -> 87.8 us (0.988)
  Pallas kernels: 87.3 us -> 86.2 us
    pallas_call x1, Pallas kernels: 83 us -> 81.9 us  [local(): pl.pallas_call(functools.partial(exchange, dims, slots, total), name='exc...]
where the time goes in v4:
time: 87.8 us; the launch traced here: 87.5 us
  Pallas kernels  86.2 us (98%)
  between operations  1.29 us (1%)
    pallas_call x1, Pallas kernels, local(): pl.pallas_call(functools.partial(exchange, dims, slots, total), name='exc...  81.9 us
    pallas_call x1, Pallas kernels, local(): pl.pallas_call(orthonormal, name='orthonormal', out_shape=(jax.ShapeDtype...  4.33 us

profile of v4, /device:TPU:1, one launch (start us, length us, event | category | flops | bytes accessed | tf_op | source)
XLA Modules:
  0.0 87.5 jit_solution(3522920239233605275)
XLA Ops:
  1.3 81.9 %exchange.1 = (f32[32,128]{1,0:T(8,128)}, f32[64,256]{1,0:T(8,128)}) custom-call(s32[2,24]{1,0:T(2,128)} %bitcast.1, s32[1]{0:T(128)S(6)} %copy.6.counts, bf16[64,256]{1,0:T(8,128)(2,1)} %x_hbm.1, bf16[24,256,256]{2,1,0:T(8,128)(2,1)} %tiles_hbm.1), custom_call_target="tpu_custom_call" | custom-call | tf_op jit(solution)/shard_map/exchange/pallas_call | solution.py:416
  83.2 4.3 %orthonormal.1 = (f32[64,256]{1,0:T(8,128)}, f32[64,64]{1,0:T(8,128)}) custom-call(f32[32,128]{1,0:T(8,128)} %get-tuple-element.4.gram_ref, f32[64,256]{1,0:T(8,128)} %get-tuple-element.5.y_hbm), custom_call_target="tpu_custom_call" | custom-call | tf_op jit(solution)/shard_map/orthonormal/pallas_call | solution.py:456
